TPU v7x, 512 devices: a whole 4x8x8 slice. The times are simulated.
512 devices in a mesh: section: 16 (over z, core), expert: 16 (over x_lo, y), dp: 2 (over x_hi).
Axes of the slice: x: 4 (x_hi: 2, x_lo: 2; x = x_hi * 2 + x_lo), y: 8, z: 8, core: 2. Of those that a mesh axis runs over, the one named last changes fastest.
Arguments:
- acts: bfloat16 [16, 4096, 1536], P('section', ('expert', 'dp')), may hold values from -6 to 6
- norm_gain: float32 [16, 1536], P('section'), may hold values from 0.1 to 1.9
- w_gate: bfloat16 [16, 1536, 6144], P('section', None, 'expert'), may hold values from -0.15625 to 0.15625
- w_up: bfloat16 [16, 1536, 6144], P('section', None, 'expert'), may hold values from -0.15625 to 0.15625
- w_down: bfloat16 [16, 6144, 1536], P('section', 'expert'), may hold values from -0.15625 to 0.15625
- routes: int32 [2, 16, 4096, 2], P(None, 'section', ('expert', 'dp')), may hold values from 0 to 3, all different within a row; in each aligned block of 128 rows (0 to 127, 128 to 255, ..., all dimensions but the last counted through in order) at most 66 rows name the same one
- gates: float32 [2, 16, 4096, 2], P(None, 'section', ('expert', 'dp')), may hold values from 0.2 to 1
Outputs:
- out: bfloat16 [16, 4096, 1536], P('section', ('expert', 'dp'))
Inputs may be any that keep to these rules, and one draw needn't show every extreme that they name: `routes`: each row names 2 different experts. Within the rows of one device at one visit (aligned blocks of 128 rows) no expert is named by more than 66 rows, a bound that some block reaches.
All inputs are finite; a program needn't handle non-finite values.
Results may differ from a plain program's by a relative error of at most 0.0065.
Values may be sent and summed in bfloat16 or wider, within the bound.
A program may use at most 64 MiB of HBM per device.

v0:
```python
import jax
import jax.numpy as jnp
from jax import lax
from jax.sharding import PartitionSpec as P

D = 1536
EXPERTS = 4
TOP = 2
STOPS = 2
TOK_DEV = 128
CAP = 66


epsilon = 1e-05


def passed_along(block, axis, distance):
    devices = range(lax.axis_size(axis))
    route = [((i - distance) % len(devices), i) for i in devices]
    return lax.ppermute(block, axis, route)


def body(acts, norm_gain, w_gate, w_up, w_down, routes, gates):
    owners = lax.axis_size("expert")
    slab_count = owners // EXPERTS
    gain_row = norm_gain[0]
    gate_cols = w_gate[0]
    up_cols = w_up[0]
    down_rows = w_down[0]
    current = acts[0]
    for stop_index in range(STOPS):
        current = passed_along(current, "section", 1)
        widened = current.astype(jnp.float32)
        scale_row = lax.rsqrt(jnp.mean(widened * widened, axis=-1, keepdims=True) + epsilon)
        normed = (widened * scale_row * gain_row).astype(jnp.bfloat16)
        flat_route = routes[stop_index, 0].reshape(-1)
        onehot = (flat_route[:, None] == jnp.arange(EXPERTS, dtype=jnp.int32)[None, :]).astype(
            jnp.int32
        )
        before = (jnp.cumsum(onehot, axis=0) - onehot) * onehot
        slot_of = jnp.sum(before, axis=1)
        repeated = jnp.repeat(normed, TOP, axis=0)
        blocks = jnp.zeros((EXPERTS, CAP, D), jnp.bfloat16).at[flat_route, slot_of].set(repeated)
        copies = jnp.broadcast_to(blocks[:, None], (EXPERTS, slab_count, CAP, D))
        outbox = copies.reshape(owners, CAP, D)
        received = lax.all_to_all(outbox, "expert", split_axis=0, concat_axis=0, tiled=True)
        flat_rows = received.reshape(-1, received.shape[2])
        gate_pre = jnp.dot(flat_rows, gate_cols, preferred_element_type=jnp.float32)
        up_pre = jnp.dot(flat_rows, up_cols, preferred_element_type=jnp.float32)
        hidden = (jax.nn.silu(gate_pre) * up_pre).astype(jnp.bfloat16)
        partial_value = jnp.dot(hidden, down_rows, preferred_element_type=jnp.float32).astype(
            jnp.bfloat16
        )
        returned = lax.all_to_all(
            partial_value.reshape(received.shape), "expert", split_axis=0, concat_axis=0, tiled=True
        )
        returned = returned.reshape(EXPERTS, slab_count, CAP, D)
        picked = (
            returned[flat_route, :, slot_of]
            .astype(jnp.float32)
            .sum(axis=1)
            .reshape(TOK_DEV, TOP, D)
        )
        mixture = jnp.sum(picked * gates[stop_index, 0][..., None], axis=1)
        current = (widened + mixture).astype(jnp.bfloat16)
    return current[None]


def solution(mesh):
    placed = (
        P("section", ("expert", "dp"), None),
        P("section", None),
        P("section", None, "expert"),
        P("section", None, "expert"),
        P("section", "expert", None),
        P(None, "section", ("expert", "dp"), None),
        P(None, "section", ("expert", "dp"), None),
    )
    return jax.shard_map(
        body,
        mesh=mesh,
        in_specs=placed,
        out_specs=P("section", ("expert", "dp"), None),
        check_vma=False,
    )
```

profile of v0, /device:TPU:175, one launch (start us, length us, event | category | flops | bytes accessed | tf_op | source)
XLA Modules:
  0.0 524.7 jit_solution(4022363407360172533)
XLA Ops:
  9.8 30.0 %scatter_fusion = bf16[4,66,1536]{2,0,1:T(4,128)(2,1)S(1)} fusion(bf16[4,66,1536]{2,0,1:T(4,128)(2,1)S(1)} %broadcast.127.clone, s32[256]{0:T(256)S(1)} %bitcast.91, bf16[256,1536]{1,0:T(8,128)(2,1)} %reshape.200), kind=kCustom, calls=%fused_computation.2 | custom fusion | bytes 2361344 | tf_op jit(solution)/shard_map/scatter | solution.py:43
  40.3 85.4 %all_to_all.20 = bf16[16,66,1536]{2,1,0:T(8,128)(2,1)} all-to-all(bf16[16,66,1536]{2,1,0:T(8,128)(2,1)S(1)} %bitcast.94), channel_id=1, replica_groups=mesh['section'=16,'expert'=16,'dp'=2] {'expert'}, dimensions={0} | all-to-all | bytes 6488064 | tf_op jit(solution)/shard_map/all_to_all | solution.py:46
  125.7 4.8 reshape.175
  130.5 4.9 fusion.8
  135.4 8.0 %convolution_convert_fusion.1 = bf16[1056,1536]{1,0:T(8,128)(2,1)} fusion(bf16[1,384,1536]{2,1,0:T(8,128)(2,1)S(1)} %copy-done, bf16[1056,1536]{1,0:T(8,128)(2,1)} %reshape.175, f32[1056,384]{1,0:T(8,128)} %fusion.8, bf16[1,1536,384]{2,1,0:T(8,128)(2,1)} %param.10), kind=kOutput, calls=%fused_computation.5 | convolution fusion | flops 2495471616 | bytes 10469376 | tf_op jit(solution)/shard_map/dot_general | solution.py:51
  143.4 4.6 reshape.176
  148.0 7.6 %all-to-all-start.1 = ((bf16[16,66,1536]{2,1,0:T(8,128)(2,1)}), bf16[16,66,1536]{2,1,0:T(8,128)(2,1)}, u32[]{:S(2)}, u32[]{:S(2)}) async-start(bf16[16,66,1536]{2,1,0:T(8,128)(2,1)} %reshape.176), calls=%async_computation.1 | async-start | bytes 7077888 | tf_op jit(solution)/shard_map/all_to_all | solution.py:54
  157.6 76.1 %all-to-all-done.1 = bf16[16,66,1536]{2,1,0:T(8,128)(2,1)} async-done(((bf16[16,66,1536]{2,1,0:T(8,128)(2,1)}), bf16[16,66,1536]{2,1,0:T(8,128)(2,1)}, u32[]{:S(2)}, u32[]{:S(2)}) %all-to-all-start.1) | async-done | bytes 3244064 | tf_op jit(solution)/shard_map/all_to_all | solution.py:54
  233.7 5.4 %copy.71 = bf16[4,4,66,1536]{3,1,2,0:T(4,128)(2,1)} copy(bf16[4,4,66,1536]{3,2,1,0:T(8,128)(2,1)} %bitcast.9) | data formatting | bytes 6488064 | tf_op jit(solution)/shard_map/reshape | solution.py:57
  239.0 7.1 %gather_fusion = bf16[256,4,1536]{2,1,0:T(4,128)(2,1)} fusion(bf16[4,4,66,1536]{3,1,2,0:T(4,128)(2,1)} %copy.71, s32[256]{0:T(256)S(1)} %bitcast.92), kind=kCustom, calls=%fused_computation | custom fusion | bytes 6293504 | tf_op jit(solution)/shard_map/gather | solution.py:59
  246.1 7.5 %convert_reduce_fusion.1 = f32[256,1536]{1,0:T(8,128)} fusion(bf16[256,4,1536]{2,1,0:T(4,128)(2,1)} %gather_fusion), kind=kLoop, calls=%fused_computation.7 | loop fusion | flops 2752512 | bytes 4718592 | tf_op jit(solution)/shard_map/reduce_sum | solution.py:61
  258.2 9.8 %collective-permute-start.1 = (bf16[128,1536]{1,0:T(8,128)(2,1)S(1)}, bf16[128,1536]{1,0:T(8,128)(2,1)S(1)}, u32[]{:S(2)}, u32[]{:S(2)}) collective-permute-start(bf16[128,1536]{1,0:T(8,128)(2,1)S(1)} %fusion.19), channel_id=1, source_target_pairs={{480,0},{0,32},{32,64},{64,96},{96,128},{128,160},{160,192},{192,2... | collective-permute-start | bytes 1179656 | tf_op jit(solution)/shard_map/ppermute | solution.py:20
  268.4 4.3 collective-permute-done.1
  274.9 30.0 %scatter_fusion.1 = bf16[4,66,1536]{2,0,1:T(4,128)(2,1)S(1)} fusion(bf16[4,66,1536]{2,0,1:T(4,128)(2,1)S(1)} %broadcast.127, s32[256]{0:T(256)S(1)} %bitcast.90, bf16[256,1536]{1,0:T(8,128)(2,1)} %reshape.206), kind=kCustom, calls=%fused_computation.3 | custom fusion | bytes 2361344 | tf_op jit(solution)/shard_map/scatter | solution.py:43
  305.3 80.8 %all_to_all.21 = bf16[16,66,1536]{2,1,0:T(8,128)(2,1)} all-to-all(bf16[16,66,1536]{2,1,0:T(8,128)(2,1)S(1)} %bitcast.95), channel_id=1, replica_groups=mesh['section'=16,'expert'=16,'dp'=2] {'expert'}, dimensions={0} | all-to-all | bytes 6488064 | tf_op jit(solution)/shard_map/all_to_all | solution.py:46
  386.1 4.8 reshape.182
  390.9 4.9 fusion.6
  395.8 8.0 %convolution_convert_fusion = bf16[1056,1536]{1,0:T(8,128)(2,1)} fusion(bf16[1,384,1536]{2,1,0:T(8,128)(2,1)S(1)} %copy-done, bf16[1056,1536]{1,0:T(8,128)(2,1)} %reshape.182, f32[1056,384]{1,0:T(8,128)} %fusion.6, bf16[1,1536,384]{2,1,0:T(8,128)(2,1)} %param.10), kind=kOutput, calls=%fused_computation.4 | convolution fusion | flops 2495471616 | bytes 10469376 | tf_op jit(solution)/shard_map/dot_general | solution.py:51
  403.8 4.6 reshape.183
  408.4 7.6 %all-to-all-start.3 = ((bf16[16,66,1536]{2,1,0:T(8,128)(2,1)}), bf16[16,66,1536]{2,1,0:T(8,128)(2,1)}, u32[]{:S(2)}, u32[]{:S(2)}) async-start(bf16[16,66,1536]{2,1,0:T(8,128)(2,1)} %reshape.183), calls=%async_computation.3 | async-start | bytes 7077888 | tf_op jit(solution)/shard_map/all_to_all | solution.py:54
  416.1 83.2 %all-to-all-done.3 = bf16[16,66,1536]{2,1,0:T(8,128)(2,1)} async-done(((bf16[16,66,1536]{2,1,0:T(8,128)(2,1)}), bf16[16,66,1536]{2,1,0:T(8,128)(2,1)}, u32[]{:S(2)}, u32[]{:S(2)}) %all-to-all-start.3) | async-done | bytes 3244064 | tf_op jit(solution)/shard_map/all_to_all | solution.py:54
  499.3 5.4 %copy.81 = bf16[4,4,66,1536]{3,1,2,0:T(4,128)(2,1)} copy(bf16[4,4,66,1536]{3,2,1,0:T(8,128)(2,1)} %bitcast.17) | data formatting | bytes 6488064 | tf_op jit(solution)/shard_map/reshape | solution.py:57
  504.7 7.1 %gather_fusion.1 = bf16[256,4,1536]{2,1,0:T(4,128)(2,1)} fusion(bf16[4,4,66,1536]{3,1,2,0:T(4,128)(2,1)} %copy.81, s32[256]{0:T(256)S(1)} %bitcast.93), kind=kCustom, calls=%fused_computation.1 | custom fusion | bytes 6293504 | tf_op jit(solution)/shard_map/gather | solution.py:59
  511.7 7.5 %convert_reduce_fusion = f32[256,1536]{1,0:T(8,128)} fusion(bf16[256,4,1536]{2,1,0:T(4,128)(2,1)} %gather_fusion.1), kind=kLoop, calls=%fused_computation.6 | loop fusion | flops 2752512 | bytes 4718592 | tf_op jit(solution)/shard_map/reduce_sum | solution.py:61
  (65 shorter events, 25.0 us)
Async XLA Ops:
  0.0 135.4 %copy-start = (bf16[1,384,1536]{2,1,0:T(8,128)(2,1)S(1)}, bf16[1,384,1536]{2,1,0:T(8,128)(2,1)}, u32[]{:S(2)}) copy-start(bf16[1,384,1536]{2,1,0:T(8,128)(2,1)} %param.11) | copy-start | bytes 3538948
  0.0 7.7 %collective-permute-start = (bf16[128,1536]{1,0:T(8,128)(2,1)}, bf16[128,1536]{1,0:T(8,128)(2,1)S(1)}, u32[]{:S(2)}, u32[]{:S(2)}) collective-permute-start(bf16[128,1536]{1,0:T(8,128)(2,1)} %bitcast.100), channel_id=1, source_target_pairs={{480,0},{0,32},{32,64},{64,96},{96,128},{128,160},{160,192},{192,2... | collective-permute-start | bytes 1179656 | tf_op jit(solution)/shard_map/ppermute | solution.py:20
  125.7 4.8 copy-start.2
  148.0 7.6 %copy-start.1 = (f32[2,1,128,2]{2,3,1,0:T(2,128)S(1)}, f32[2,1,128,2]{2,3,1,0:T(2,128)}, u32[]{:S(2)}) copy-start(f32[2,1,128,2]{2,3,1,0:T(2,128)} %param.13) | copy-start | bytes 6148
  148.0 85.7 %all-to-all-start.1 = ((bf16[16,66,1536]{2,1,0:T(8,128)(2,1)}), bf16[16,66,1536]{2,1,0:T(8,128)(2,1)}, u32[]{:S(2)}, u32[]{:S(2)}) async-start(bf16[16,66,1536]{2,1,0:T(8,128)(2,1)} %reshape.176), calls=%async_computation.1 | async-start | bytes 7077888 | tf_op jit(solution)/shard_map/all_to_all | solution.py:54
  258.2 14.5 %collective-permute-start.1 = (bf16[128,1536]{1,0:T(8,128)(2,1)S(1)}, bf16[128,1536]{1,0:T(8,128)(2,1)S(1)}, u32[]{:S(2)}, u32[]{:S(2)}) collective-permute-start(bf16[128,1536]{1,0:T(8,128)(2,1)S(1)} %fusion.19), channel_id=1, source_target_pairs={{480,0},{0,32},{32,64},{64,96},{96,128},{128,160},{160,192},{192,2... | collective-permute-start | bytes 1179656 | tf_op jit(solution)/shard_map/ppermute | solution.py:20
  386.1 4.8 copy-start.3
  408.4 90.9 %all-to-all-start.3 = ((bf16[16,66,1536]{2,1,0:T(8,128)(2,1)}), bf16[16,66,1536]{2,1,0:T(8,128)(2,1)}, u32[]{:S(2)}, u32[]{:S(2)}) async-start(bf16[16,66,1536]{2,1,0:T(8,128)(2,1)} %reshape.183), calls=%async_computation.3 | async-start | bytes 7077888 | tf_op jit(solution)/shard_map/all_to_all | solution.py:54
where the time goes:
time: 533 us; the launch traced here: 525 us
  blocking collectives  166 us (31%)
  waiting for transfers between devices  165 us (31%)
  local copies, waits for them, and re-layouts  115 us (22%)
  starting transfers between devices  27.6 us (5%)
  matrix products  25.8 us (5%)
  other arithmetic  24.3 us (5%)
    all_to_all x2, blocking collectives, body(): lax.all_to_all(outbox, 'expert', split_axis=0, concat_axis=0, tiled=True)  166 us
    all_to_all x2, waiting for transfers between devices, body(): lax.all_to_all(partial_value.reshape(received.shape), 'expert', split_axi...  159 us
    scatter x4, local copies, waits for them, and re-layouts, body(): jnp.zeros((EXPERTS, CAP, D), jnp.bfloat16).at[flat_route, slot_of]  60.3 us
    dot_general x2, matrix products, body(): jnp.dot(hidden, down_rows, preferred_element_type=jnp.float32)  16 us
    all_to_all x2, starting transfers between devices, body(): lax.all_to_all(partial_value.reshape(received.shape), 'expert', split_axi...  15.2 us
    reduce_sum x2, other arithmetic, body(): picked = returned[flat_route, :, slot_of].astype(jnp.float32).sum(axis=1)...  14.9 us
    gather x2, local copies, waits for them, and re-layouts, body(): returned[flat_route, :, slot_of].astype(jnp.float32).sum(axis=1)  14.2 us
    ppermute x2, starting transfers between devices, passed_along(): return lax.ppermute(block, axis, route)  12.4 us
  transfers between devices with their start and end apart: 4, of which 4 were waited for; matrix products, arithmetic and copies ran while one was open for 1% of the time, Pallas kernels for 0%

commit v1 on v0

v1 whole, which is shorter than its diff:
```python
import jax
import jax.numpy as jnp
from jax import lax
from jax.sharding import PartitionSpec as P

D = 1536
EXPERTS = 4
STOPS = 2

epsilon = 1e-05


def passed_along(block, axis, distance):
    devices = range(lax.axis_size(axis))
    route = [((i - distance) % len(devices), i) for i in devices]
    return lax.ppermute(block, axis, route)


def body(acts, norm_gain, w_gate, w_up, w_down, routes, gates):
    slab_count = lax.axis_size("expert") // EXPERTS
    mine = lax.axis_index("expert") // slab_count
    gain_row = norm_gain[0]
    gate_cols = w_gate[0]
    up_cols = w_up[0]
    down_rows = w_down[0]
    current = acts[0]
    dense = jnp.sum(
        jnp.where(
            routes[:, 0, :, :, None] == jnp.arange(EXPERTS, dtype=jnp.int32),
            gates[:, 0, :, :, None],
            0.0,
        ),
        axis=2,
    )
    every = lax.all_gather(dense, "expert", axis=1, tiled=True)
    column = jnp.sum(
        jnp.where(jnp.arange(EXPERTS, dtype=jnp.int32) == mine, every, 0.0), axis=2, keepdims=True
    )
    for stop_index in range(STOPS):
        current = passed_along(current, "section", 1)
        widened = current.astype(jnp.float32)
        scale_row = lax.rsqrt(jnp.mean(widened * widened, axis=-1, keepdims=True) + epsilon)
        normed = (widened * scale_row * gain_row).astype(jnp.bfloat16)
        rows = lax.all_gather(normed, "expert", axis=0, tiled=True)
        gate_pre = jnp.dot(rows, gate_cols, preferred_element_type=jnp.float32)
        up_pre = jnp.dot(rows, up_cols, preferred_element_type=jnp.float32)
        hidden = (jax.nn.silu(gate_pre) * up_pre).astype(jnp.bfloat16)
        partial_value = jnp.dot(hidden, down_rows, preferred_element_type=jnp.float32)
        weighted = (partial_value * column[stop_index]).astype(jnp.bfloat16)
        mixture = lax.psum_scatter(weighted, "expert", scatter_dimension=0, tiled=True)
        current = (widened + mixture.astype(jnp.float32)).astype(jnp.bfloat16)
    return current[None]


def solution(mesh):
    placed = (
        P("section", ("expert", "dp"), None),
        P("section", None),
        P("section", None, "expert"),
        P("section", None, "expert"),
        P("section", "expert", None),
        P(None, "section", ("expert", "dp"), None),
        P(None, "section", ("expert", "dp"), None),
    )
    return jax.shard_map(
        body,
        mesh=mesh,
        in_specs=placed,
        out_specs=P("section", ("expert", "dp"), None),
        check_vma=False,
    )
```

time: 533 us -> 419 us (0.79)
  the two profiles are of different devices: /device:TPU:175 before, /device:TPU:4 now
where the time goes in v1:
time: 419 us
  waiting for transfers between devices  326 us (78%)
  matrix products  38.2 us (9%)
  blocking collectives  34 us (8%)
  between operations  13.2 us (3%)
  other arithmetic  6.79 us (2%)
    reduce_scatter x2, waiting for transfers between devices, body(): lax.psum_scatter(weighted, 'expert', scatter_dimension=0, tiled=True)  174 us
    all_gather x2, waiting for transfers between devices, body(): rows = lax.all_gather(normed, 'expert', axis=0, tiled=True)  131 us
    all_gather x1, blocking collectives, body(): every = lax.all_gather(dense, 'expert', axis=1, tiled=True)  34 us
    dot_general x2, matrix products, body(): jnp.dot(hidden, down_rows, preferred_element_type=jnp.float32)  22.2 us
    ppermute x2, waiting for transfers between devices, passed_along(): return lax.ppermute(block, axis, route)  21.7 us
    dot_general x2, matrix products, body(): gate_pre = jnp.dot(rows, gate_cols, preferred_element_type=jnp.float32)  16.1 us
  transfers between devices with their start and end apart: 6, of which 6 were waited for; matrix products, arithmetic and copies ran while one was open for 0% of the time, Pallas kernels for 0%

profile of v1, /device:TPU:4, one launch (start us, length us, event | category | flops | bytes accessed | tf_op | source)
XLA Modules:
  0.0 418.7 jit_solution(3023250668859743433)
XLA Ops:
  6.5 0.8 reduce
  7.4 13.3 %collective-permute-done = bf16[128,1536]{1,0:T(8,128)(2,1)S(1)} collective-permute-done((bf16[128,1536]{1,0:T(8,128)(2,1)}, bf16[128,1536]{1,0:T(8,128)(2,1)S(1)}, u32[]{:S(2)}, u32[]{:S(2)}) %collective-permute-start) | collective-permute-done | bytes 393248 | tf_op jit(solution)/shard_map/ppermute | solution.py:16
  20.7 0.2 fusion.12
  20.9 0.9 fusion.14
  21.8 0.0 reduce-scatter.3.cloned.1.call-start
  21.9 0.7 select_reduce_fusion.1
  22.6 34.0 %all_gather.10 = f32[2,2048,4]{1,2,0:T(4,128)S(1)} all-gather(f32[2,128,4]{1,2,0:T(4,128)S(1)} %select_reduce_fusion.1), channel_id=1, replica_groups=mesh['section'=16,'expert'=16,'dp'=2] {'expert'}, dimensions={1}, use_global_device_ids=true | all-gather | bytes 69632 | tf_op jit(solution)/shard_map/all_gather | solution.py:35
  56.6 0.1 select_reduce_fusion
  56.8 48.9 %all-gather.3.cloned.1.call-done = bf16[2048,1536]{1,0:T(8,128)(2,1)} async-done(((bf16[128,1536]{1,0:T(8,128)(2,1)}), bf16[2048,1536]{1,0:T(8,128)(2,1)}) %all-gather.3.cloned.1.call-update) | async-done | bytes 6291472 | tf_op jit(solution)/shard_map/all_gather | solution.py:44
  105.6 8.2 %fusion.6 = f32[2048,384]{1,0:T(8,128)} fusion(bf16[2048,1536]{1,0:T(8,128)(2,1)} %all-gather.3.cloned.1.call-done, bf16[1,1536,384]{2,1,0:T(8,128)(2,1)} %param.9), kind=kOutput, calls=%fused_computation.16 | convolution fusion | flops 2415919104 | bytes 10616832 | tf_op jit(solution)/shard_map/dot_general | solution.py:45
  113.8 10.9 %multiply_convert_fusion.1 = bf16[2048,1536]{1,0:T(8,128)(2,1)} fusion(f32[2048]{0:T(1024)S(1)} %bitcast.31, bf16[1,384,1536]{2,1,0:T(8,128)(2,1)S(1)} %copy-done, f32[2048,384]{1,0:T(8,128)} %fusion.6, bf16[2048,1536]{1,0:T(8,128)(2,1)} %all-gather.3.cloned.1.call-done, bf16[1,1536,384]{2,1,0:T(8,128)(2,1)S(1)} %copy-done.2), kind=kOutput, calls=%fused_computation.1 | convolution fusion | flops 4842848256 | bytes 18096128 | tf_op jit(solution)/shard_map/dot_general | solution.py:48
  124.8 0.0 all-gather.5.cloned.1.call-start
  124.8 86.9 %reduce-scatter.3.cloned.1.call-done = bf16[128,1536]{1,0:T(8,128)(2,1)} async-done(((bf16[2048,1536]{1,0:T(8,128)(2,1)}), bf16[128,1536]{1,0:T(8,128)(2,1)}) %reduce-scatter.3.cloned.1.call-update) | async-done | bytes 393232 | tf_op jit(solution)/shard_map/reduce_scatter | solution.py:50
  211.7 1.1 fusion.15
  212.8 0.0 collective-permute-start.1
  212.8 8.4 %collective-permute-done.1 = bf16[128,1536]{1,0:T(8,128)(2,1)S(1)} collective-permute-done((bf16[128,1536]{1,0:T(8,128)(2,1)S(1)}, bf16[128,1536]{1,0:T(8,128)(2,1)S(1)}, u32[]{:S(2)}, u32[]{:S(2)}) %collective-permute-start.1) | collective-permute-done | bytes 393248 | tf_op jit(solution)/shard_map/ppermute | solution.py:16
  221.2 0.2 fusion.16
  221.4 0.9 fusion.18
  222.3 0.0 reduce-scatter.5.cloned.1.call-start
  222.4 81.8 %all-gather.5.cloned.1.call-done = bf16[2048,1536]{1,0:T(8,128)(2,1)} async-done(((bf16[128,1536]{1,0:T(8,128)(2,1)}), bf16[2048,1536]{1,0:T(8,128)(2,1)}) %all-gather.5.cloned.1.call-update) | async-done | bytes 6291472 | tf_op jit(solution)/shard_map/all_gather | solution.py:44
  304.2 7.9 %fusion.4 = f32[2048,384]{1,0:T(8,128)} fusion(bf16[2048,1536]{1,0:T(8,128)(2,1)} %all-gather.5.cloned.1.call-done, bf16[1,1536,384]{2,1,0:T(8,128)(2,1)S(1)} %copy-done.1), kind=kOutput, calls=%fused_computation.14 | convolution fusion | flops 2415919104 | bytes 10616832 | tf_op jit(solution)/shard_map/dot_general | solution.py:45
  312.1 11.3 %multiply_convert_fusion = bf16[2048,1536]{1,0:T(8,128)(2,1)} fusion(f32[2048]{0:T(1024)S(1)} %bitcast.30, bf16[1,384,1536]{2,1,0:T(8,128)(2,1)S(1)} %copy-done, f32[2048,384]{1,0:T(8,128)} %fusion.4, bf16[2048,1536]{1,0:T(8,128)(2,1)} %all-gather.5.cloned.1.call-done, bf16[1,1536,384]{2,1,0:T(8,128)(2,1)} %param.10), kind=kOutput, calls=%fused_computation | convolution fusion | flops 4842848256 | bytes 18096128 | tf_op jit(solution)/shard_map/dot_general | solution.py:48
  323.4 86.9 %reduce-scatter.5.cloned.1.call-done = bf16[128,1536]{1,0:T(8,128)(2,1)} async-done(((bf16[2048,1536]{1,0:T(8,128)(2,1)}), bf16[128,1536]{1,0:T(8,128)(2,1)}) %reduce-scatter.5.cloned.1.call-update) | async-done | bytes 393232 | tf_op jit(solution)/shard_map/reduce_scatter | solution.py:50
  410.3 1.9 fusion.20
  (16 shorter events, 0.1 us)
Async XLA Ops:
  6.5 107.3 %copy-start = (bf16[1,384,1536]{2,1,0:T(8,128)(2,1)S(1)}, bf16[1,384,1536]{2,1,0:T(8,128)(2,1)}, u32[]{:S(2)}) copy-start(bf16[1,384,1536]{2,1,0:T(8,128)(2,1)} %param.11) | copy-start | bytes 3538948
  6.5 99.1 %all-gather.3.cloned.1.call-start = ((), (), s32[]{:S(2)}) async-start(), calls=%async_computation.2 | async-start | bytes 6684672 | tf_op jit(solution)/shard_map/all_gather | solution.py:44
  6.5 14.1 %collective-permute-start = (bf16[128,1536]{1,0:T(8,128)(2,1)}, bf16[128,1536]{1,0:T(8,128)(2,1)S(1)}, u32[]{:S(2)}, u32[]{:S(2)}) collective-permute-start(bf16[128,1536]{1,0:T(8,128)(2,1)} %bitcast.34), channel_id=1, source_target_pairs={{480,0},{0,32},{32,64},{64,96},{96,128},{128,160},{160,192},{192,2... | collective-permute-start | bytes 1179656 | tf_op jit(solution)/shard_map/ppermute | solution.py:16
  21.8 189.9 %reduce-scatter.3.cloned.1.call-start = ((), (), s32[]{:S(2)}) async-start(), calls=%async_computation.3 | async-start | bytes 6684672 | tf_op jit(solution)/shard_map/reduce_scatter | solution.py:50
  56.8 57.1 %copy-start.2 = (bf16[1,1536,384]{2,1,0:T(8,128)(2,1)S(1)}, bf16[1,1536,384]{2,1,0:T(8,128)(2,1)}, u32[]{:S(2)}) copy-start(bf16[1,1536,384]{2,1,0:T(8,128)(2,1)} %param.10) | copy-start | bytes 3538948
  124.7 179.5 %copy-start.1 = (bf16[1,1536,384]{2,1,0:T(8,128)(2,1)S(1)}, bf16[1,1536,384]{2,1,0:T(8,128)(2,1)}, u32[]{:S(2)}) copy-start(bf16[1,1536,384]{2,1,0:T(8,128)(2,1)} %param.9) | copy-start | bytes 3538948
  124.8 179.5 %all-gather.5.cloned.1.call-start = ((), (), s32[]{:S(2)}) async-start(), calls=%async_computation.4 | async-start | bytes 6684672 | tf_op jit(solution)/shard_map/all_gather | solution.py:44
  212.8 8.4 %collective-permute-start.1 = (bf16[128,1536]{1,0:T(8,128)(2,1)S(1)}, bf16[128,1536]{1,0:T(8,128)(2,1)S(1)}, u32[]{:S(2)}, u32[]{:S(2)}) collective-permute-start(bf16[128,1536]{1,0:T(8,128)(2,1)S(1)} %fusion.15), channel_id=1, source_target_pairs={{480,0},{0,32},{32,64},{64,96},{96,128},{128,160},{160,192},{192,2... | collective-permute-start | bytes 1179656 | tf_op jit(solution)/shard_map/ppermute | solution.py:16
  222.3 188.0 %reduce-scatter.5.cloned.1.call-start = ((), (), s32[]{:S(2)}) async-start(), calls=%async_computation.5 | async-start | bytes 6684672 | tf_op jit(solution)/shard_map/reduce_scatter | solution.py:50
Sparse Core Ops, SparseCore 0:
  21.9 83.6 all-gather.2
  124.9 86.7 reduce-scatter.2
  222.5 81.6 all-gather.4
  323.5 86.7 reduce-scatter.4

commit v2 on v1

v2 whole, which is shorter than its diff:
```python
import jax
import jax.numpy as jnp
import numpy as np
from jax import lax
from jax.experimental import pallas as pl
from jax.experimental.pallas import tpu as pltpu
from jax.sharding import PartitionSpec as P

D = 1536
EXPERTS = 4
STOPS = 2
RING = 8
HALF = 64

epsilon = 1e-05

FLOWS = (
    ("a", 1, 4, 0),
    ("a", -1, 3, 0),
    ("a", 1, 3, 1),
    ("a", -1, 4, 1),
    ("b", 1, 4, 0),
    ("b", -1, 3, 0),
)
B_FLOWS = (4, 5)

SLOT = {"a0": 0, "an0": 1, "b0": 2, "bx0": 3}
SOURCE = [(0, 0, 0), (1, 0, 0), (0, 0, 1), (1, 0, 1)]
GROUPS = [(0, 1)]
for _k in range(1, 5):
    _first = len(SOURCE)
    for _f, (_b, _s, _n, _o) in enumerate(FLOWS):
        if _k <= _n:
            SLOT[(_f, _k)] = len(SOURCE)
            SOURCE.append((_o, _s * _k, int(_b == "b")))
    for _f in B_FLOWS:
        if _k <= FLOWS[_f][2]:
            SLOT[("x", _f, _k)] = len(SOURCE)
            SOURCE.append((1, FLOWS[_f][1] * _k, 1))
    GROUPS.append((_first // 4, len(SOURCE) // 4))
SLOTS = len(SOURCE)

BACK = {}
for _f, _flow in enumerate(FLOWS):
    for _k in range(_flow[2]):
        BACK[(_f, _k)] = len(BACK)
for _f in B_FLOWS:
    for _k in range(1, FLOWS[_f][2] + 1):
        BACK[("x", _f, _k)] = len(BACK)
BACK["bx0"] = len(BACK)
BACK["ax0"] = len(BACK)
BACKS = len(BACK)


def visit_kernel(
    x_ref, col_ref, wg_ref, wu_ref, wd_ref, out_ref,
    rows, part, stage, back, send_sem, recv_sem, bsend_sem, brecv_sem,
):
    me = lax.axis_index("expert")
    ring = me // RING
    y = me % RING
    turn = 1 - 2 * (lax.axis_index("section") % 2)
    ahead = ring * RING + (y + turn + RING) % RING
    behind = ring * RING + (y - turn + RING) % RING
    across = (1 - ring) * RING + y

    barrier = pltpu.get_barrier_semaphore()
    for peer in (ahead, behind, across):
        pl.semaphore_signal(
            barrier, inc=1, device_id={"expert": peer}, device_id_type=pl.DeviceIdType.MESH
        )
    pl.semaphore_wait(barrier, 3)

    own = {"a": x_ref.at[pl.ds(0, HALF)], "b": x_ref.at[pl.ds(HALF, HALF)]}
    sent = []

    def send(source, slot, peer):
        copy = pltpu.make_async_remote_copy(
            src_ref=source,
            dst_ref=rows.at[slot],
            send_sem=send_sem.at[slot],
            recv_sem=recv_sem.at[slot],
            device_id={"expert": peer},
            device_id_type=pl.DeviceIdType.MESH,
        )
        copy.start()
        sent.append(copy)
        return copy

    def give(slot, place, peer):
        copy = pltpu.make_async_remote_copy(
            src_ref=stage.at[slot],
            dst_ref=back.at[place],
            send_sem=bsend_sem.at[place],
            recv_sem=brecv_sem.at[place],
            device_id={"expert": peer},
            device_id_type=pl.DeviceIdType.MESH,
        )
        copy.start()
        sent.append(copy)
        return copy

    def compute(group):
        def chunk(c, carry):
            x = rows[pl.ds(c * 4, 4)].reshape(4 * HALF, D)
            g = jnp.dot(x, wg_ref[...], preferred_element_type=jnp.float32)
            u = jnp.dot(x, wu_ref[...], preferred_element_type=jnp.float32)
            h = (g / (1.0 + jnp.exp(-g)) * u).astype(jnp.bfloat16)
            p = jnp.dot(h, wd_ref[...], preferred_element_type=jnp.float32)
            w = col_ref[pl.ds(c * 4, 4)].reshape(4 * HALF, 1)
            part[pl.ds(c * 4, 4)] = (p * w).reshape(4, HALF, D)
            return carry

        lax.fori_loop(GROUPS[group][0], GROUPS[group][1], chunk, 0)

    flight = {}
    home = {}

    def across_back(slot, place):
        stage[slot] = part[slot].astype(jnp.bfloat16)
        home[place] = give(slot, BACK[place], across)

    flight["an0"] = send(own["a"], SLOT["an0"], across)
    for f in (0, 1, 4, 5):
        block, sign, _, _ = FLOWS[f]
        flight[(f, 1)] = send(own[block], SLOT[(f, 1)], ahead if sign > 0 else behind)
    flight["bx0"] = send(own["b"], SLOT["bx0"], across)
    rows[SLOT["a0"]] = x_ref[pl.ds(0, HALF)]
    rows[SLOT["b0"]] = x_ref[pl.ds(HALF, HALF)]
    flight["an0"].wait_recv()
    for f in (2, 3):
        flight[(f, 1)] = send(
            rows.at[SLOT["an0"]], SLOT[(f, 1)], ahead if FLOWS[f][1] > 0 else behind
        )
    flight["bx0"].wait_recv()
    compute(0)
    across_back(SLOT["bx0"], "bx0")
    for k in range(1, 5):
        for f in (4, 5, 0, 1, 2, 3):
            _, sign, hops, _ = FLOWS[f]
            if k > hops:
                continue
            flight[(f, k)].wait_recv()
            if k < hops:
                flight[(f, k + 1)] = send(
                    rows.at[SLOT[(f, k)]], SLOT[(f, k + 1)], ahead if sign > 0 else behind
                )
            if f in B_FLOWS:
                flight[("x", f, k)] = send(rows.at[SLOT[(f, k)]], SLOT[("x", f, k)], across)
        for f in B_FLOWS:
            if k <= FLOWS[f][2]:
                flight[("x", f, k)].wait_recv()
        compute(k)
        for f in B_FLOWS:
            if k <= FLOWS[f][2]:
                across_back(SLOT[("x", f, k)], ("x", f, k))

    for k in range(4, 0, -1):
        order = (1, 2, 0, 3, 5, 4) if k == 3 else (0, 3, 1, 2, 4, 5)
        for f in order:
            _, sign, hops, _ = FLOWS[f]
            if k > hops:
                continue
            total = part[SLOT[(f, k)]]
            if f in B_FLOWS:
                home[("x", f, k)].wait_recv()
                total = total + back[BACK[("x", f, k)]].astype(jnp.float32)
            if k < hops:
                home[(f, k)].wait_recv()
                total = total + back[BACK[(f, k)]].astype(jnp.float32)
            stage[SLOT[(f, k)]] = total.astype(jnp.bfloat16)
            home[(f, k - 1)] = give(
                SLOT[(f, k)], BACK[(f, k - 1)], behind if sign > 0 else ahead
            )

    def gathered(slot, places):
        total = part[slot]
        for place in places:
            home[place].wait_recv()
            total = total + back[BACK[place]].astype(jnp.float32)
        return total

    stage[SLOT["an0"]] = gathered(SLOT["an0"], [(2, 0), (3, 0)]).astype(jnp.bfloat16)
    home["ax0"] = give(SLOT["an0"], BACK["ax0"], across)
    out_ref[pl.ds(HALF, HALF)] = gathered(SLOT["b0"], ["bx0", (4, 0), (5, 0)])
    out_ref[pl.ds(0, HALF)] = gathered(SLOT["a0"], [(0, 0), (1, 0), "ax0"])
    for copy in sent:
        copy.wait_send()


def visit(normed, col, wg, wu, wd):
    vmem = pl.BlockSpec(memory_space=pltpu.VMEM)
    return pl.pallas_call(
        visit_kernel,
        out_shape=jax.ShapeDtypeStruct((2 * HALF, D), jnp.float32),
        in_specs=[vmem] * 5,
        out_specs=vmem,
        scratch_shapes=[
            pltpu.VMEM((SLOTS, HALF, D), jnp.bfloat16),
            pltpu.VMEM((SLOTS, HALF, D), jnp.float32),
            pltpu.VMEM((SLOTS, HALF, D), jnp.bfloat16),
            pltpu.VMEM((BACKS, HALF, D), jnp.bfloat16),
            pltpu.SemaphoreType.DMA((SLOTS,)),
            pltpu.SemaphoreType.DMA((SLOTS,)),
            pltpu.SemaphoreType.DMA((BACKS,)),
            pltpu.SemaphoreType.DMA((BACKS,)),
        ],
        compiler_params=pltpu.CompilerParams(
            collective_id=0, has_side_effects=True, vmem_limit_bytes=60 * 1024 * 1024
        ),
    )(normed, col, wg, wu, wd)


def passed_along(block, axis, distance):
    devices = range(lax.axis_size(axis))
    route = [((i - distance) % len(devices), i) for i in devices]
    return lax.ppermute(block, axis, route)


def body(acts, norm_gain, w_gate, w_up, w_down, routes, gates):
    me = lax.axis_index("expert")
    mine = me // (lax.axis_size("expert") // EXPERTS)
    gain_row = norm_gain[0]
    current = acts[0]
    experts = jnp.arange(EXPERTS, dtype=jnp.int32)
    dense = jnp.sum(
        jnp.where(routes[:, 0, :, :, None] == experts, gates[:, 0, :, :, None], 0.0), axis=2
    )
    every = lax.all_gather(dense, "expert", axis=1, tiled=True)
    column = jnp.sum(jnp.where(experts == mine, every, 0.0), axis=2)
    table = np.array(SOURCE, dtype=np.int32)
    turn = 1 - 2 * (lax.axis_index("section") % 2)
    source = (me // RING + table[:, 0]) % 2 * RING + (me % RING - turn * table[:, 1] + RING) % RING
    column = column.reshape(STOPS, 4 * RING, HALF)
    column = jnp.take(column, source * 2 + table[:, 2], axis=1)[..., None]
    for stop_index in range(STOPS):
        current = passed_along(current, "section", 1)
        widened = current.astype(jnp.float32)
        scale_row = lax.rsqrt(jnp.mean(widened * widened, axis=-1, keepdims=True) + epsilon)
        normed = (widened * scale_row * gain_row).astype(jnp.bfloat16)
        mixture = visit(normed, column[stop_index], w_gate[0], w_up[0], w_down[0])
        current = (widened + mixture).astype(jnp.bfloat16)
    return current[None]


def solution(mesh):
    placed = (
        P("section", ("expert", "dp"), None),
        P("section", None),
        P("section", None, "expert"),
        P("section", None, "expert"),
        P("section", "expert", None),
        P(None, "section", ("expert", "dp"), None),
        P(None, "section", ("expert", "dp"), None),
    )
    return jax.shard_map(
        body,
        mesh=mesh,
        in_specs=placed,
        out_specs=P("section", ("expert", "dp"), None),
        check_vma=False,
    )
```

time: 419 us -> 317 us (0.76)
  the two profiles are of different devices: /device:TPU:4 before, /device:TPU:192 now
where the time goes in v2:
time: 317 us; the launch traced here: 316 us
  Pallas kernels  265 us (84%)
  blocking collectives  34.2 us (11%)
  other arithmetic  6.99 us (2%)
  waiting for transfers between devices  5.79 us (2%)
  local copies, waits for them, and re-layouts  3.56 us (1%)
    pallas_call x2, Pallas kernels, visit(): pl.pallas_call(visit_kernel, out_shape=jax.ShapeDtypeStruct((2 * HALF, D)...  265 us
    all_gather x1, blocking collectives, body(): every = lax.all_gather(dense, 'expert', axis=1, tiled=True)  34.2 us
  transfers between devices with their start and end apart: 2, of which 1 were waited for; matrix products, arithmetic and copies ran while one was open for 2% of the time, Pallas kernels for 0%

profile of v2, /device:TPU:192, one launch (start us, length us, event | category | flops | bytes accessed | tf_op | source)
XLA Modules:
  0.0 316.1 jit_solution(16449080785756191432)
XLA Ops:
  0.0 0.0 copy-start
  0.0 0.0 collective-permute-start
  0.0 0.7 compare_and_fusion
  0.8 0.7 select_reduce_fusion.1
  1.5 34.2 %all_gather.3 = f32[2,2048,4]{1,2,0:T(4,128)S(1)} all-gather(f32[2,128,4]{1,2,0:T(4,128)S(1)} %select_reduce_fusion.1), channel_id=1, replica_groups=mesh['section'=16,'expert'=16,'dp'=2] {'expert'}, dimensions={1}, use_global_device_ids=true | all-gather | bytes 69632 | tf_op jit(solution)/shard_map/all_gather | solution.py:229
  35.7 0.1 select_reduce_fusion
  35.8 0.1 reshape.30
  35.9 0.6 gather_fusion
  36.6 0.1 select_bitcast_fusion
  36.7 1.4 copy.24.col_ref
  38.1 0.0 copy-done
  38.1 0.0 collective-permute-done
  38.1 0.2 fusion
  38.3 0.9 fusion.2.x_ref
  39.2 122.9 %shard_map.100 = f32[128,1536]{1,0:T(8,128)} custom-call(bf16[128,1536]{1,0:T(8,128)(2,1)} %fusion.2.x_ref, f32[32,64,1]{2,1,0:T(8,128)} %copy.24.col_ref, bf16[1536,384]{1,0:T(8,128)(2,1)} %bitcast.12, bf16[1536,384]{1,0:T(8,128)(2,1)} %bitcast.14, bf16[384,1536]{1,0:T(8,128)(2,1)} %bitcast.16), custom_call_target="tpu_custom_call" | custom-call | tf_op jit(solution)/shard_map/pallas_call | solution.py:193
  162.2 1.2 fusion.3
  163.4 0.0 collective-permute-start.1
  163.4 1.4 copy.25.col_ref
  164.8 5.8 %collective-permute-done.1 = bf16[128,1536]{1,0:T(8,128)(2,1)S(1)} collective-permute-done((bf16[128,1536]{1,0:T(8,128)(2,1)S(1)}, bf16[128,1536]{1,0:T(8,128)(2,1)S(1)}, u32[]{:S(2)}, u32[]{:S(2)}) %collective-permute-start.1) | collective-permute-done | bytes 393248 | tf_op jit(solution)/shard_map/ppermute | solution.py:217
  170.6 0.2 fusion.4
  170.7 0.9 fusion.6.x_ref
  171.7 142.5 %shard_map.101 = f32[128,1536]{1,0:T(8,128)} custom-call(bf16[128,1536]{1,0:T(8,128)(2,1)} %fusion.6.x_ref, f32[32,64,1]{2,1,0:T(8,128)} %copy.25.col_ref, bf16[1536,384]{1,0:T(8,128)(2,1)} %bitcast.13, bf16[1536,384]{1,0:T(8,128)(2,1)} %bitcast.15, bf16[384,1536]{1,0:T(8,128)(2,1)} %bitcast.17), custom_call_target="tpu_custom_call" | custom-call | tf_op jit(solution)/shard_map/pallas_call | solution.py:193
  314.2 1.9 fusion.8
  (7 shorter events, 0.1 us)
Async XLA Ops:
  0.0 38.1 %copy-start = (f32[1,1536]{1,0:T(1,128)S(1)}, f32[1,1536]{1,0:T(1,128)}, u32[]{:S(2)}) copy-start(f32[1,1536]{1,0:T(1,128)} %param.11) | copy-start | bytes 18436
  0.0 38.1 %collective-permute-start = (bf16[128,1536]{1,0:T(8,128)(2,1)}, bf16[128,1536]{1,0:T(8,128)(2,1)S(1)}, u32[]{:S(2)}, u32[]{:S(2)}) collective-permute-start(bf16[128,1536]{1,0:T(8,128)(2,1)} %bitcast.22), channel_id=1, source_target_pairs={{480,0},{0,32},{32,64},{64,96},{96,128},{128,160},{160,192},{192,2... | collective-permute-start | bytes 1179656 | tf_op jit(solution)/shard_map/ppermute | solution.py:217
  163.4 7.2 %collective-permute-start.1 = (bf16[128,1536]{1,0:T(8,128)(2,1)S(1)}, bf16[128,1536]{1,0:T(8,128)(2,1)S(1)}, u32[]{:S(2)}, u32[]{:S(2)}) collective-permute-start(bf16[128,1536]{1,0:T(8,128)(2,1)S(1)} %fusion.3), channel_id=1, source_target_pairs={{480,0},{0,32},{32,64},{64,96},{96,128},{128,160},{160,192},{192,2... | collective-permute-start | bytes 1179656 | tf_op jit(solution)/shard_map/ppermute | solution.py:217

commit v3 on v2

--- a/solution.py
+++ b/solution.py
@@ -100,18 +100,18 @@
         sent.append(copy)
         return copy
 
-    def compute(group):
-        def chunk(c, carry):
-            x = rows[pl.ds(c * 4, 4)].reshape(4 * HALF, D)
+    def compute(c):
+        def chunk(i, carry):
+            x = rows[pl.ds(i * 4, 4)].reshape(4 * HALF, D)
             g = jnp.dot(x, wg_ref[...], preferred_element_type=jnp.float32)
             u = jnp.dot(x, wu_ref[...], preferred_element_type=jnp.float32)
             h = (g / (1.0 + jnp.exp(-g)) * u).astype(jnp.bfloat16)
             p = jnp.dot(h, wd_ref[...], preferred_element_type=jnp.float32)
-            w = col_ref[pl.ds(c * 4, 4)].reshape(4 * HALF, 1)
-            part[pl.ds(c * 4, 4)] = (p * w).reshape(4, HALF, D)
+            w = col_ref[pl.ds(i * 4, 4)].reshape(4 * HALF, 1)
+            part[pl.ds(i * 4, 4)] = (p * w).reshape(4, HALF, D)
             return carry
 
-        lax.fori_loop(GROUPS[group][0], GROUPS[group][1], chunk, 0)
+        lax.fori_loop(c, c + 1, chunk, 0)
 
     flight = {}
     home = {}
@@ -132,46 +132,61 @@
         flight[(f, 1)] = send(
             rows.at[SLOT["an0"]], SLOT[(f, 1)], ahead if FLOWS[f][1] > 0 else behind
         )
-    flight["bx0"].wait_recv()
-    compute(0)
+    def returned(f, k):
+        _, sign, hops, _ = FLOWS[f]
+        total = part[SLOT[(f, k)]]
+        if f in B_FLOWS:
+            home[("x", f, k)].wait_recv()
+            total = total + back[BACK[("x", f, k)]].astype(jnp.float32)
+        if k < hops:
+            home[(f, k)].wait_recv()
+            total = total + back[BACK[(f, k)]].astype(jnp.float32)
+        stage[SLOT[(f, k)]] = total.astype(jnp.bfloat16)
+        home[(f, k - 1)] = give(SLOT[(f, k)], BACK[(f, k - 1)], behind if sign > 0 else ahead)
+
+    for k in range(1, 5):
+        waiting = list(range(*GROUPS[k - 1]))
+        for pair in ((4, 5), (0, 1), (2, 3)):
+            for f in pair:
+                _, sign, hops, _ = FLOWS[f]
+                if k > hops:
+                    continue
+                flight[(f, k)].wait_recv()
+                if k < hops:
+                    flight[(f, k + 1)] = send(
+                        rows.at[SLOT[(f, k)]], SLOT[(f, k + 1)], ahead if sign > 0 else behind
+                    )
+                if f in B_FLOWS:
+                    flight[("x", f, k)] = send(rows.at[SLOT[(f, k)]], SLOT[("x", f, k)], across)
+            if waiting and pair != (2, 3):
+                if k == 1:
+                    flight["bx0"].wait_recv()
+                else:
+                    for f in B_FLOWS:
+                        if pair == (4, 5):
+                            flight[("x", f, k - 1)].wait_recv()
+                compute(waiting.pop(0))
+    for f in B_FLOWS:
+        across_back(SLOT[("x", f, 3)], ("x", f, 3))
+    returned(1, 3)
+    returned(2, 3)
+    flight[("x", 4, 4)].wait_recv()
+    compute(GROUPS[4][0])
+    across_back(SLOT[("x", 4, 4)], ("x", 4, 4))
+    returned(0, 4)
+    returned(3, 4)
+    returned(5, 3)
+    for k in (2, 1):
+        for f in B_FLOWS:
+            across_back(SLOT[("x", f, k)], ("x", f, k))
     across_back(SLOT["bx0"], "bx0")
-    for k in range(1, 5):
-        for f in (4, 5, 0, 1, 2, 3):
-            _, sign, hops, _ = FLOWS[f]
-            if k > hops:
-                continue
-            flight[(f, k)].wait_recv()
-            if k < hops:
-                flight[(f, k + 1)] = send(
-                    rows.at[SLOT[(f, k)]], SLOT[(f, k + 1)], ahead if sign > 0 else behind
-                )
-            if f in B_FLOWS:
-                flight[("x", f, k)] = send(rows.at[SLOT[(f, k)]], SLOT[("x", f, k)], across)
-        for f in B_FLOWS:
-            if k <= FLOWS[f][2]:
-                flight[("x", f, k)].wait_recv()
-        compute(k)
-        for f in B_FLOWS:
-            if k <= FLOWS[f][2]:
-                across_back(SLOT[("x", f, k)], ("x", f, k))
-
-    for k in range(4, 0, -1):
-        order = (1, 2, 0, 3, 5, 4) if k == 3 else (0, 3, 1, 2, 4, 5)
-        for f in order:
-            _, sign, hops, _ = FLOWS[f]
-            if k > hops:
-                continue
-            total = part[SLOT[(f, k)]]
-            if f in B_FLOWS:
-                home[("x", f, k)].wait_recv()
-                total = total + back[BACK[("x", f, k)]].astype(jnp.float32)
-            if k < hops:
-                home[(f, k)].wait_recv()
-                total = total + back[BACK[(f, k)]].astype(jnp.float32)
-            stage[SLOT[(f, k)]] = total.astype(jnp.bfloat16)
-            home[(f, k - 1)] = give(
-                SLOT[(f, k)], BACK[(f, k - 1)], behind if sign > 0 else ahead
-            )
+
+    returned(4, 4)
+    for f in (0, 3, 4):
+        returned(f, 3)
+    for k in (2, 1):
+        for f in (1, 2, 5, 0, 3, 4):
+            returned(f, k)
 
     def gathered(slot, places):
         total = part[slot]
@@ -219,18 +234,15 @@
 
 def body(acts, norm_gain, w_gate, w_up, w_down, routes, gates):
     me = lax.axis_index("expert")
-    mine = me // (lax.axis_size("expert") // EXPERTS)
     gain_row = norm_gain[0]
     current = acts[0]
-    experts = jnp.arange(EXPERTS, dtype=jnp.int32)
-    dense = jnp.sum(
-        jnp.where(routes[:, 0, :, :, None] == experts, gates[:, 0, :, :, None], 0.0), axis=2
-    )
-    every = lax.all_gather(dense, "expert", axis=1, tiled=True)
-    column = jnp.sum(jnp.where(experts == mine, every, 0.0), axis=2)
+    named = jnp.arange(4 * EXPERTS, dtype=jnp.int32)[:, None, None, None] // EXPERTS
+    dense = jnp.sum(jnp.where(routes[None, :, 0] == named, gates[None, :, 0], 0.0), axis=3)
+    column = lax.all_to_all(dense, "expert", split_axis=0, concat_axis=0, tiled=True)
     table = np.array(SOURCE, dtype=np.int32)
     turn = 1 - 2 * (lax.axis_index("section") % 2)
     source = (me // RING + table[:, 0]) % 2 * RING + (me % RING - turn * table[:, 1] + RING) % RING
+    column = column.reshape(2 * RING, STOPS, 2, HALF).transpose(1, 0, 2, 3)
     column = column.reshape(STOPS, 4 * RING, HALF)
     column = jnp.take(column, source * 2 + table[:, 2], axis=1)[..., None]
     for stop_index in range(STOPS):

time: 317 us -> 250 us (0.79)
  Pallas kernels: 265 us -> 216 us
  blocking collectives: 34.2 us -> 0 us
  starting transfers between devices: 0.02 us -> 8.17 us
  waiting for transfers between devices: 5.79 us -> 12.8 us
    pallas_call x2, Pallas kernels: 265 us -> 216 us  [visit(): pl.pallas_call(visit_kernel, out_shape=jax.ShapeDtypeStruct((2 * HALF, D)...]
    all_gather x1 -> x0, blocking collectives: 34.2 us -> none  [body(): every = lax.all_gather(dense, 'expert', axis=1, tiled=True)]
    all_to_all x0 -> x1, starting transfers between devices: none -> 8.13 us  [body(): lax.all_to_all(dense, 'expert', split_axis=0, concat_axis=0, tiled=True)]
    all_to_all x0 -> x1, waiting for transfers between devices: none -> 6.98 us  [body(): lax.all_to_all(dense, 'expert', split_axis=0, concat_axis=0, tiled=True)]
  transfers between devices with their start and end apart: 2 -> 3, of which waited for: 1 -> 2; matrix products, arithmetic and copies ran while one was open for 2% -> 2% of each run, Pallas kernels for 0% -> 0%
where the time goes in v3:
time: 250 us; the launch traced here: 249 us
  Pallas kernels  216 us (86%)
  waiting for transfers between devices  12.8 us (5%)
  starting transfers between devices  8.17 us (3%)
  other arithmetic  7.62 us (3%)
  local copies, waits for them, and re-layouts  4.19 us (2%)
    pallas_call x2, Pallas kernels, visit(): pl.pallas_call(visit_kernel, out_shape=jax.ShapeDtypeStruct((2 * HALF, D)...  216 us
    all_to_all x1, starting transfers between devices, body(): lax.all_to_all(dense, 'expert', split_axis=0, concat_axis=0, tiled=True)  8.13 us
    all_to_all x1, waiting for transfers between devices, body(): lax.all_to_all(dense, 'expert', split_axis=0, concat_axis=0, tiled=True)  6.98 us
    ppermute x2, waiting for transfers between devices, passed_along(): return lax.ppermute(block, axis, route)  5.79 us
  transfers between devices with their start and end apart: 3, of which 2 were waited for; matrix products, arithmetic and copies ran while one was open for 2% of the time, Pallas kernels for 0%

profile of v3, /device:TPU:192, one launch (start us, length us, event | category | flops | bytes accessed | tf_op | source)
XLA Modules:
  0.0 249.4 jit_solution(18440095233768283303)
XLA Ops:
  0.0 0.8 select_reduce_fusion
  0.8 0.6 copy.30
  1.4 8.1 %all-to-all-start = ((f32[16,2,128]{2,1,0:T(2,128)}), f32[16,2,128]{2,1,0:T(2,128)S(1)}, u32[]{:S(2)}, u32[]{:S(2)}) async-start(f32[16,2,128]{2,1,0:T(2,128)} %copy.30), calls=%async_computation | async-start | bytes 32768 | tf_op jit(solution)/shard_map/all_to_all | solution.py:241
  9.5 0.0 collective-permute-start
  9.6 0.7 compare_and_fusion
  10.3 0.7 reduce
  11.0 7.0 %all-to-all-done = f32[16,2,128]{2,1,0:T(2,128)S(1)} async-done(((f32[16,2,128]{2,1,0:T(2,128)}), f32[16,2,128]{2,1,0:T(2,128)S(1)}, u32[]{:S(2)}, u32[]{:S(2)}) %all-to-all-start) | async-done | bytes 16416 | tf_op jit(solution)/shard_map/all_to_all | solution.py:241
  18.0 0.1 reshape.70
  18.2 0.6 gather_fusion
  18.8 0.1 select_bitcast_fusion
  18.9 1.4 copy.33.col_ref
  20.3 0.0 collective-permute-done
  20.3 0.2 fusion
  20.5 0.9 fusion.2.x_ref
  21.4 107.7 %shard_map.100 = f32[128,1536]{1,0:T(8,128)} custom-call(bf16[128,1536]{1,0:T(8,128)(2,1)} %fusion.2.x_ref, f32[32,64,1]{2,1,0:T(8,128)} %copy.33.col_ref, bf16[1536,384]{1,0:T(8,128)(2,1)} %bitcast.15, bf16[1536,384]{1,0:T(8,128)(2,1)} %bitcast.17, bf16[384,1536]{1,0:T(8,128)(2,1)} %bitcast.19), custom_call_target="tpu_custom_call" | custom-call | tf_op jit(solution)/shard_map/pallas_call | solution.py:208
  129.1 1.2 fusion.3
  130.3 0.0 collective-permute-start.1
  130.3 1.4 copy.34.col_ref
  131.7 5.8 %collective-permute-done.1 = bf16[128,1536]{1,0:T(8,128)(2,1)S(1)} collective-permute-done((bf16[128,1536]{1,0:T(8,128)(2,1)S(1)}, bf16[128,1536]{1,0:T(8,128)(2,1)S(1)}, u32[]{:S(2)}, u32[]{:S(2)}) %collective-permute-start.1) | collective-permute-done | bytes 393248 | tf_op jit(solution)/shard_map/ppermute | solution.py:232
  137.5 0.2 fusion.4
  137.7 0.9 fusion.6.x_ref
  138.6 108.8 %shard_map.101 = f32[128,1536]{1,0:T(8,128)} custom-call(bf16[128,1536]{1,0:T(8,128)(2,1)} %fusion.6.x_ref, f32[32,64,1]{2,1,0:T(8,128)} %copy.34.col_ref, bf16[1536,384]{1,0:T(8,128)(2,1)} %bitcast.16, bf16[1536,384]{1,0:T(8,128)(2,1)} %bitcast.18, bf16[384,1536]{1,0:T(8,128)(2,1)} %bitcast.20), custom_call_target="tpu_custom_call" | custom-call | tf_op jit(solution)/shard_map/pallas_call | solution.py:208
  247.4 1.9 fusion.8
  (7 shorter events, 0.1 us)
Async XLA Ops:
  1.4 16.6 %all-to-all-start = ((f32[16,2,128]{2,1,0:T(2,128)}), f32[16,2,128]{2,1,0:T(2,128)S(1)}, u32[]{:S(2)}, u32[]{:S(2)}) async-start(f32[16,2,128]{2,1,0:T(2,128)} %copy.30), calls=%async_computation | async-start | bytes 32768 | tf_op jit(solution)/shard_map/all_to_all | solution.py:241
  9.5 10.8 %collective-permute-start = (bf16[128,1536]{1,0:T(8,128)(2,1)}, bf16[128,1536]{1,0:T(8,128)(2,1)S(1)}, u32[]{:S(2)}, u32[]{:S(2)}) collective-permute-start(bf16[128,1536]{1,0:T(8,128)(2,1)} %bitcast.26), channel_id=1, source_target_pairs={{480,0},{0,32},{32,64},{64,96},{96,128},{128,160},{160,192},{192,2... | collective-permute-start | bytes 1179656 | tf_op jit(solution)/shard_map/ppermute | solution.py:232
  130.3 7.2 %collective-permute-start.1 = (bf16[128,1536]{1,0:T(8,128)(2,1)S(1)}, bf16[128,1536]{1,0:T(8,128)(2,1)S(1)}, u32[]{:S(2)}, u32[]{:S(2)}) collective-permute-start(bf16[128,1536]{1,0:T(8,128)(2,1)S(1)} %fusion.3), channel_id=1, source_target_pairs={{480,0},{0,32},{32,64},{64,96},{96,128},{128,160},{160,192},{192,2... | collective-permute-start | bytes 1179656 | tf_op jit(solution)/shard_map/ppermute | solution.py:232

commit v4 on v3

--- a/solution.py
+++ b/solution.py
@@ -121,7 +121,7 @@
         home[place] = give(slot, BACK[place], across)
 
     flight["an0"] = send(own["a"], SLOT["an0"], across)
-    for f in (0, 1, 4, 5):
+    for f in (4, 5, 0, 1):
         block, sign, _, _ = FLOWS[f]
         flight[(f, 1)] = send(own[block], SLOT[(f, 1)], ahead if sign > 0 else behind)
     flight["bx0"] = send(own["b"], SLOT["bx0"], across)
@@ -173,8 +173,8 @@
     flight[("x", 4, 4)].wait_recv()
     compute(GROUPS[4][0])
     across_back(SLOT[("x", 4, 4)], ("x", 4, 4))
+    returned(3, 4)
     returned(0, 4)
-    returned(3, 4)
     returned(5, 3)
     for k in (2, 1):
         for f in B_FLOWS:
@@ -182,10 +182,10 @@
     across_back(SLOT["bx0"], "bx0")
 
     returned(4, 4)
-    for f in (0, 3, 4):
+    for f in (3, 0, 4):
         returned(f, 3)
     for k in (2, 1):
-        for f in (1, 2, 5, 0, 3, 4):
+        for f in (2, 3, 0, 1, 4, 5):
             returned(f, k)
 
     def gathered(slot, places):

time: 250 us -> 244 us (0.976)
  Pallas kernels: 216 us -> 211 us
    pallas_call x2, Pallas kernels: 216 us -> 211 us  [visit(): pl.pallas_call(visit_kernel, out_shape=jax.ShapeDtypeStruct((2 * HALF, D)...]
where the time goes in v4:
time: 244 us
  Pallas kernels  211 us (86%)
  waiting for transfers between devices  12.8 us (5%)
  starting transfers between devices  8.17 us (3%)
  other arithmetic  7.62 us (3%)
  local copies, waits for them, and re-layouts  4.19 us (2%)
    pallas_call x2, Pallas kernels, visit(): pl.pallas_call(visit_kernel, out_shape=jax.ShapeDtypeStruct((2 * HALF, D)...  211 us
    all_to_all x1, starting transfers between devices, body(): lax.all_to_all(dense, 'expert', split_axis=0, concat_axis=0, tiled=True)  8.13 us
    all_to_all x1, waiting for transfers between devices, body(): lax.all_to_all(dense, 'expert', split_axis=0, concat_axis=0, tiled=True)  6.98 us
    ppermute x2, waiting for transfers between devices, passed_along(): return lax.ppermute(block, axis, route)  5.79 us
  transfers between devices with their start and end apart: 3, of which 2 were waited for; matrix products, arithmetic and copies ran while one was open for 2% of the time, Pallas kernels for 0%

profile of v4, /device:TPU:192, one launch (start us, length us, event | category | flops | bytes accessed | tf_op | source)
XLA Modules:
  0.0 243.6 jit_solution(2064390508450237925)
XLA Ops:
  0.0 0.8 select_reduce_fusion
  0.8 0.6 copy.30
  1.4 8.1 %all-to-all-start = ((f32[16,2,128]{2,1,0:T(2,128)}), f32[16,2,128]{2,1,0:T(2,128)S(1)}, u32[]{:S(2)}, u32[]{:S(2)}) async-start(f32[16,2,128]{2,1,0:T(2,128)} %copy.30), calls=%async_computation | async-start | bytes 32768 | tf_op jit(solution)/shard_map/all_to_all | solution.py:241
  9.5 0.0 collective-permute-start
  9.6 0.7 compare_and_fusion
  10.3 0.7 reduce
  11.0 7.0 %all-to-all-done = f32[16,2,128]{2,1,0:T(2,128)S(1)} async-done(((f32[16,2,128]{2,1,0:T(2,128)}), f32[16,2,128]{2,1,0:T(2,128)S(1)}, u32[]{:S(2)}, u32[]{:S(2)}) %all-to-all-start) | async-done | bytes 16416 | tf_op jit(solution)/shard_map/all_to_all | solution.py:241
  18.0 0.1 reshape.70
  18.2 0.6 gather_fusion
  18.8 0.1 select_bitcast_fusion
  18.9 1.4 copy.33.col_ref
  20.3 0.0 collective-permute-done
  20.3 0.2 fusion
  20.5 0.9 fusion.2.x_ref
  21.4 104.6 %shard_map.100 = f32[128,1536]{1,0:T(8,128)} custom-call(bf16[128,1536]{1,0:T(8,128)(2,1)} %fusion.2.x_ref, f32[32,64,1]{2,1,0:T(8,128)} %copy.33.col_ref, bf16[1536,384]{1,0:T(8,128)(2,1)} %bitcast.15, bf16[1536,384]{1,0:T(8,128)(2,1)} %bitcast.17, bf16[384,1536]{1,0:T(8,128)(2,1)} %bitcast.19), custom_call_target="tpu_custom_call" | custom-call | tf_op jit(solution)/shard_map/pallas_call | solution.py:208
  126.0 1.2 fusion.3
  127.2 0.0 collective-permute-start.1
  127.2 1.4 copy.34.col_ref
  128.6 5.8 %collective-permute-done.1 = bf16[128,1536]{1,0:T(8,128)(2,1)S(1)} collective-permute-done((bf16[128,1536]{1,0:T(8,128)(2,1)S(1)}, bf16[128,1536]{1,0:T(8,128)(2,1)S(1)}, u32[]{:S(2)}, u32[]{:S(2)}) %collective-permute-start.1) | collective-permute-done | bytes 393248 | tf_op jit(solution)/shard_map/ppermute | solution.py:232
  134.4 0.2 fusion.4
  134.6 0.9 fusion.6.x_ref
  135.5 106.1 %shard_map.101 = f32[128,1536]{1,0:T(8,128)} custom-call(bf16[128,1536]{1,0:T(8,128)(2,1)} %fusion.6.x_ref, f32[32,64,1]{2,1,0:T(8,128)} %copy.34.col_ref, bf16[1536,384]{1,0:T(8,128)(2,1)} %bitcast.16, bf16[1536,384]{1,0:T(8,128)(2,1)} %bitcast.18, bf16[384,1536]{1,0:T(8,128)(2,1)} %bitcast.20), custom_call_target="tpu_custom_call" | custom-call | tf_op jit(solution)/shard_map/pallas_call | solution.py:208
  241.6 1.9 fusion.8
  (7 shorter events, 0.1 us)
Async XLA Ops:
  1.4 16.6 %all-to-all-start = ((f32[16,2,128]{2,1,0:T(2,128)}), f32[16,2,128]{2,1,0:T(2,128)S(1)}, u32[]{:S(2)}, u32[]{:S(2)}) async-start(f32[16,2,128]{2,1,0:T(2,128)} %copy.30), calls=%async_computation | async-start | bytes 32768 | tf_op jit(solution)/shard_map/all_to_all | solution.py:241
  9.5 10.8 %collective-permute-start = (bf16[128,1536]{1,0:T(8,128)(2,1)}, bf16[128,1536]{1,0:T(8,128)(2,1)S(1)}, u32[]{:S(2)}, u32[]{:S(2)}) collective-permute-start(bf16[128,1536]{1,0:T(8,128)(2,1)} %bitcast.26), channel_id=1, source_target_pairs={{480,0},{0,32},{32,64},{64,96},{96,128},{128,160},{160,192},{192,2... | collective-permute-start | bytes 1179656 | tf_op jit(solution)/shard_map/ppermute | solution.py:232
  127.2 7.2 %collective-permute-start.1 = (bf16[128,1536]{1,0:T(8,128)(2,1)S(1)}, bf16[128,1536]{1,0:T(8,128)(2,1)S(1)}, u32[]{:S(2)}, u32[]{:S(2)}) collective-permute-start(bf16[128,1536]{1,0:T(8,128)(2,1)S(1)} %fusion.3), channel_id=1, source_target_pairs={{480,0},{0,32},{32,64},{64,96},{96,128},{128,160},{160,192},{192,2... | collective-permute-start | bytes 1179656 | tf_op jit(solution)/shard_map/ppermute | solution.py:232

commit v5 on v4

--- a/solution.py
+++ b/solution.py
@@ -53,9 +53,18 @@
 
 
 def visit_kernel(
-    x_ref, col_ref, wg_ref, wu_ref, wd_ref, out_ref,
-    rows, part, stage, back, send_sem, recv_sem, bsend_sem, brecv_sem,
+    x_ref, moved_ref, col_ref, wg_hbm, wu_hbm, wd_hbm, out_ref,
+    rows, part, stage, back, wg_ref, wu_ref, wd_ref,
+    send_sem, recv_sem, bsend_sem, brecv_sem, weight_sem,
 ):
+    weights = [
+        pltpu.make_async_copy(source, held, weight_sem.at[i])
+        for i, (source, held) in enumerate(
+            ((wg_hbm, wg_ref), (wu_hbm, wu_ref), (wd_hbm, wd_ref))
+        )
+    ]
+    for copy in weights:
+        copy.start()
     me = lax.axis_index("expert")
     ring = me // RING
     y = me % RING
@@ -144,6 +153,8 @@
         stage[SLOT[(f, k)]] = total.astype(jnp.bfloat16)
         home[(f, k - 1)] = give(SLOT[(f, k)], BACK[(f, k - 1)], behind if sign > 0 else ahead)
 
+    for copy in weights:
+        copy.wait()
     for k in range(1, 5):
         waiting = list(range(*GROUPS[k - 1]))
         for pair in ((4, 5), (0, 1), (2, 3)):
@@ -197,33 +208,42 @@
 
     stage[SLOT["an0"]] = gathered(SLOT["an0"], [(2, 0), (3, 0)]).astype(jnp.bfloat16)
     home["ax0"] = give(SLOT["an0"], BACK["ax0"], across)
-    out_ref[pl.ds(HALF, HALF)] = gathered(SLOT["b0"], ["bx0", (4, 0), (5, 0)])
-    out_ref[pl.ds(0, HALF)] = gathered(SLOT["a0"], [(0, 0), (1, 0), "ax0"])
+
+    def finish(first, total):
+        old = moved_ref[pl.ds(first, HALF)].astype(jnp.float32)
+        out_ref[pl.ds(first, HALF)] = (old + total).astype(jnp.bfloat16)
+
+    finish(HALF, gathered(SLOT["b0"], ["bx0", (4, 0), (5, 0)]))
+    finish(0, gathered(SLOT["a0"], [(0, 0), (1, 0), "ax0"]))
     for copy in sent:
         copy.wait_send()
 
 
-def visit(normed, col, wg, wu, wd):
+def visit(normed, moved, col, wg, wu, wd):
     vmem = pl.BlockSpec(memory_space=pltpu.VMEM)
     return pl.pallas_call(
         visit_kernel,
-        out_shape=jax.ShapeDtypeStruct((2 * HALF, D), jnp.float32),
-        in_specs=[vmem] * 5,
+        out_shape=jax.ShapeDtypeStruct((2 * HALF, D), jnp.bfloat16),
+        in_specs=[vmem] * 3 + [pl.BlockSpec(memory_space=pl.ANY)] * 3,
         out_specs=vmem,
         scratch_shapes=[
             pltpu.VMEM((SLOTS, HALF, D), jnp.bfloat16),
             pltpu.VMEM((SLOTS, HALF, D), jnp.float32),
             pltpu.VMEM((SLOTS, HALF, D), jnp.bfloat16),
             pltpu.VMEM((BACKS, HALF, D), jnp.bfloat16),
+            pltpu.VMEM(wg.shape, wg.dtype),
+            pltpu.VMEM(wu.shape, wu.dtype),
+            pltpu.VMEM(wd.shape, wd.dtype),
             pltpu.SemaphoreType.DMA((SLOTS,)),
             pltpu.SemaphoreType.DMA((SLOTS,)),
             pltpu.SemaphoreType.DMA((BACKS,)),
             pltpu.SemaphoreType.DMA((BACKS,)),
+            pltpu.SemaphoreType.DMA((3,)),
         ],
         compiler_params=pltpu.CompilerParams(
             collective_id=0, has_side_effects=True, vmem_limit_bytes=60 * 1024 * 1024
         ),
-    )(normed, col, wg, wu, wd)
+    )(normed, moved, col, wg, wu, wd)
 
 
 def passed_along(block, axis, distance):
@@ -250,8 +270,9 @@
         widened = current.astype(jnp.float32)
         scale_row = lax.rsqrt(jnp.mean(widened * widened, axis=-1, keepdims=True) + epsilon)
         normed = (widened * scale_row * gain_row).astype(jnp.bfloat16)
-        mixture = visit(normed, column[stop_index], w_gate[0], w_up[0], w_down[0])
-        current = (widened + mixture).astype(jnp.bfloat16)
+        current = visit(
+            normed, current, column[stop_index], w_gate[0], w_up[0], w_down[0]
+        )
     return current[None]
 
 

time: 244 us -> 241 us (0.988)
  other arithmetic: 7.62 us -> 4.47 us
where the time goes in v5:
time: 241 us
  Pallas kernels  209 us (87%)
  waiting for transfers between devices  13 us (5%)
  starting transfers between devices  8.17 us (3%)
  local copies, waits for them, and re-layouts  5.96 us (2%)
  other arithmetic  4.47 us (2%)
    pallas_call x2, Pallas kernels, visit(): pl.pallas_call(visit_kernel, out_shape=jax.ShapeDtypeStruct((2 * HALF, D)...  209 us
    all_to_all x1, starting transfers between devices, body(): lax.all_to_all(dense, 'expert', split_axis=0, concat_axis=0, tiled=True)  8.13 us
    all_to_all x1, waiting for transfers between devices, body(): lax.all_to_all(dense, 'expert', split_axis=0, concat_axis=0, tiled=True)  6.98 us
    ppermute x2, waiting for transfers between devices, passed_along(): return lax.ppermute(block, axis, route)  6 us
  transfers between devices with their start and end apart: 3, of which 2 were waited for; matrix products, arithmetic and copies ran while one was open for 2% of the time, Pallas kernels for 0%

profile of v5, /device:TPU:192, one launch (start us, length us, event | category | flops | bytes accessed | tf_op | source)
XLA Modules:
  0.0 240.6 jit_solution(5474330216069270666)
XLA Ops:
  0.0 0.8 select_reduce_fusion
  0.8 0.6 copy.30
  1.4 8.1 %all-to-all-start = ((f32[16,2,128]{2,1,0:T(2,128)}), f32[16,2,128]{2,1,0:T(2,128)S(1)}, u32[]{:S(2)}, u32[]{:S(2)}) async-start(f32[16,2,128]{2,1,0:T(2,128)} %copy.30), calls=%async_computation | async-start | bytes 32768 | tf_op jit(solution)/shard_map/all_to_all | solution.py:261
  9.5 0.0 collective-permute-start
  9.6 0.7 compare_and_fusion
  10.3 0.7 reduce
  11.0 7.0 %all-to-all-done = f32[16,2,128]{2,1,0:T(2,128)S(1)} async-done(((f32[16,2,128]{2,1,0:T(2,128)}), f32[16,2,128]{2,1,0:T(2,128)S(1)}, u32[]{:S(2)}, u32[]{:S(2)}) %all-to-all-start) | async-done | bytes 16416 | tf_op jit(solution)/shard_map/all_to_all | solution.py:261
  18.0 0.1 reshape.70
  18.2 0.6 gather_fusion
  18.8 0.1 select_bitcast_fusion
  18.9 1.4 copy.33.col_ref
  20.3 0.0 collective-permute-done.moved_ref
  20.3 0.2 fusion
  20.5 0.9 fusion.2.x_ref
  21.4 0.0 copy-done
  21.4 103.5 %shard_map.100 = bf16[128,1536]{1,0:T(8,128)(2,1)} custom-call(bf16[128,1536]{1,0:T(8,128)(2,1)} %fusion.2.x_ref, bf16[128,1536]{1,0:T(8,128)(2,1)} %copy-done, f32[32,64,1]{2,1,0:T(8,128)} %copy.33.col_ref, bf16[1536,384]{1,0:T(8,128)(2,1)} %bitcast.14, bf16[1536,384]{1,0:T(8,128)(2,1)} %bitcast.16, bf16[384,1536]{1,0:T(8,128)(2,1)} %bitcast.18), custom_call_target="tpu_custom_call" | custom-call | tf_op jit(solution)/shard_map/pallas_call | solution.py:224
  125.0 0.0 collective-permute-start.1
  125.0 1.4 copy.34.col_ref
  126.4 6.0 %collective-permute-done.1.moved_ref = bf16[128,1536]{1,0:T(8,128)(2,1)S(1)} collective-permute-done((bf16[128,1536]{1,0:T(8,128)(2,1)}, bf16[128,1536]{1,0:T(8,128)(2,1)S(1)}, u32[]{:S(2)}, u32[]{:S(2)}) %collective-permute-start.1) | collective-permute-done | bytes 393248 | tf_op jit(solution)/shard_map/ppermute | solution.py:252
  132.4 0.2 fusion.3
  132.6 0.9 fusion.5.x_ref
  133.5 0.0 copy-done.1
  133.5 105.3 %shard_map.101 = bf16[128,1536]{1,0:T(8,128)(2,1)} custom-call(bf16[128,1536]{1,0:T(8,128)(2,1)} %fusion.5.x_ref, bf16[128,1536]{1,0:T(8,128)(2,1)} %copy-done.1, f32[32,64,1]{2,1,0:T(8,128)} %copy.34.col_ref, bf16[1536,384]{1,0:T(8,128)(2,1)} %bitcast.15, bf16[1536,384]{1,0:T(8,128)(2,1)} %bitcast.17, bf16[384,1536]{1,0:T(8,128)(2,1)} %bitcast.19), custom_call_target="tpu_custom_call" | custom-call | tf_op jit(solution)/shard_map/pallas_call | solution.py:224
  238.8 1.8 copy.36
  (9 shorter events, 0.1 us)
Async XLA Ops:
  1.4 16.6 %all-to-all-start = ((f32[16,2,128]{2,1,0:T(2,128)}), f32[16,2,128]{2,1,0:T(2,128)S(1)}, u32[]{:S(2)}, u32[]{:S(2)}) async-start(f32[16,2,128]{2,1,0:T(2,128)} %copy.30), calls=%async_computation | async-start | bytes 32768 | tf_op jit(solution)/shard_map/all_to_all | solution.py:261
  9.5 10.8 %collective-permute-start = (bf16[128,1536]{1,0:T(8,128)(2,1)}, bf16[128,1536]{1,0:T(8,128)(2,1)S(1)}, u32[]{:S(2)}, u32[]{:S(2)}) collective-permute-start(bf16[128,1536]{1,0:T(8,128)(2,1)} %bitcast.26), channel_id=1, source_target_pairs={{480,0},{0,32},{32,64},{64,96},{96,128},{128,160},{160,192},{192,2... | collective-permute-start | bytes 1179656 | tf_op jit(solution)/shard_map/ppermute | solution.py:252
  20.3 1.1 copy-start
  125.0 7.4 %collective-permute-start.1 = (bf16[128,1536]{1,0:T(8,128)(2,1)}, bf16[128,1536]{1,0:T(8,128)(2,1)S(1)}, u32[]{:S(2)}, u32[]{:S(2)}) collective-permute-start(bf16[128,1536]{1,0:T(8,128)(2,1)} %shard_map.100), channel_id=1, source_target_pairs={{480,0},{0,32},{32,64},{64,96},{96,128},{128,160},{160,192},{192,2... | collective-permute-start | bytes 1179656 | tf_op jit(solution)/shard_map/ppermute | solution.py:252
  132.4 1.1 copy-start.1
